TPU v7x, 512 devices: a whole 4x8x8 slice. The times are simulated.
512 devices in a mesh: context: 32 (over y, x), tensor: 16 (over z, core).
Axes of the slice: x: 4, y: 8, z: 8, core: 2. Of those that a mesh axis runs over, the one named last changes fastest.
Arguments:
- queries: bfloat16 [1, 16384, 4096], P(None, 'context', 'tensor'), may hold values from -6 to 6
- keys: bfloat16 [1, 16384, 4096], P(None, 'context', 'tensor'), may hold values from -0.546875 to 0.546875
- spike_counts: int32 [1, 16384, 4096], P(None, 'context', 'tensor'), may hold values from -4 to 4
- spike_scale: float32 [4096], P('tensor'), may hold values from 0.5 to 2
- log_decay: float32 [1, 32, 16384], P(None, 'tensor', 'context'), may hold values from -3 to 0, as said below
- norm_gain: float32 [4096], P('tensor'), may hold values from 0.5 to 1.5
- out_weight: bfloat16 [4096, 8192], P('context', 'tensor'), may hold values from -0.09375 to 0.09375
- residual_in: bfloat16 [1, 16384, 8192], P(None, 'context', 'tensor'), may hold values from -6 to 6
Outputs:
- residual_out: bfloat16 [1, 16384, 8192], P(None, 'context', 'tensor')
Inputs may be any that keep to these rules, and one draw needn't show every extreme that they name: log_decay is negative.
All inputs are finite; a program needn't handle non-finite values.
Results may differ from a plain program's by a relative error of at most 0.0095.
Values may be sent and summed in bfloat16 or wider, within the bound.
A program may use at most 64 MiB of HBM per device.

v0:
```python
import jax
import jax.numpy as jnp
from jax import lax
from jax.sharding import PartitionSpec as P

epsilon = 1e-06


def prefix_2(value, axis, combine, identity):
    size, position = (lax.axis_size(axis), lax.axis_index(axis))
    everything = jax.tree.map(
        lambda part, kind: lax.all_gather(part.astype(kind), axis),
        value,
        (jnp.bfloat16, jnp.bfloat16),
    )
    start = jax.tree.map(
        lambda part, zero: jnp.broadcast_to(jnp.asarray(zero, part.dtype), part.shape),
        value,
        identity,
    )

    def lap(k, before):
        reached = k < position
        new = combine(
            before, jax.tree.map(lambda part, own: part[k].astype(own.dtype), everything, value)
        )
        return jax.tree.map(lambda a, b: jnp.where(reached, a, b), new, before)

    return lax.fori_loop(0, size, lap, start)


def combine(earlier, later):
    return (earlier[0] * later[0], later[0][..., None, None] * earlier[1] + later[1])


def local(queries, keys, spike_counts, spike_scale, log_decay, norm_gain, out_weight, residual_in):
    requests, block, width_here = queries.shape
    heads = log_decay.shape[1]
    head_size = width_here // heads
    values = (spike_counts.astype(jnp.float32) * spike_scale).astype(jnp.bfloat16)

    def split_heads(array):
        return array.reshape(requests, block, heads, head_size).transpose(0, 2, 1, 3)

    query_h = split_heads(queries)
    key_h = split_heads(keys)
    value_h = split_heads(values)
    cumulative = jnp.cumsum(log_decay, axis=2)
    vocabulary_identifiers = jnp.arange(block)
    causal = vocabulary_identifiers[:, None] >= vocabulary_identifiers[None, :]
    gaps = cumulative[..., :, None] - cumulative[..., None, :]
    decay_mat = jnp.exp(jnp.where(causal, gaps, -1e30))
    scores = jnp.einsum("rhtd,rhsd->rhts", query_h, key_h, preferred_element_type=jnp.float32)
    weights = (scores * decay_mat).astype(jnp.bfloat16)
    intra = jnp.einsum("rhts,rhsd->rhtd", weights, value_h, preferred_element_type=jnp.float32)
    to_end = jnp.exp(cumulative[..., -1:] - cumulative)
    weighted_keys = (key_h.astype(jnp.float32) * to_end[..., None]).astype(jnp.bfloat16)
    own_state = jnp.einsum(
        "rhsd,rhse->rhde", weighted_keys, value_h, preferred_element_type=jnp.float32
    )
    span_decay = jnp.exp(cumulative[..., -1])
    prefix = prefix_2(
        (span_decay, own_state),
        "context",
        combine,
        (jnp.ones_like(span_decay), jnp.zeros_like(own_state)),
    )
    incoming = prefix[1]
    carried = jnp.exp(cumulative)[..., None] * jnp.einsum(
        "rhtd,rhde->rhte", query_h.astype(jnp.float32), incoming, precision=lax.Precision.HIGHEST
    )
    mixed = intra + carried
    scale = lax.rsqrt(jnp.mean(mixed * mixed, axis=-1, keepdims=True) + epsilon)
    normed = (mixed * scale * norm_gain.reshape(1, heads, 1, head_size)).astype(jnp.bfloat16)
    normed = normed.transpose(0, 2, 1, 3).reshape(requests * block, width_here)
    all_heads = lax.all_gather(normed, "tensor", axis=1, tiled=True)
    projected = jnp.dot(
        all_heads,
        lax.all_gather(out_weight, "context", axis=0, tiled=True),
        preferred_element_type=jnp.float32,
    )
    projected = projected.reshape(requests, block, out_weight.shape[1])
    return (residual_in.astype(jnp.float32) + projected).astype(jnp.bfloat16)


def solution(mesh):
    in_specs = (
        P(None, "context", "tensor"),
        P(None, "context", "tensor"),
        P(None, "context", "tensor"),
        P("tensor"),
        P(None, "tensor", "context"),
        P("tensor"),
        P("context", "tensor"),
        P(None, "context", "tensor"),
    )
    out_specs = P(None, "context", "tensor")
    return jax.shard_map(local, mesh=mesh, in_specs=in_specs, out_specs=out_specs, check_vma=False)
```

profile of v0, /device:TPU:1, one launch (start us, length us, event | category | flops | bytes accessed | tf_op | source)
XLA Modules:
  0.0 247.4 jit_solution(11480079209673487597)
XLA Ops:
  8.4 1.1 copy.44
  9.5 1.1 multiply_convert_fusion.3
  12.7 31.4 %all-gather = bf16[32,2,1]{2,1,0:T(2,128)(2,1)S(1)} all-gather(bf16[1,2,1]{2,1,0:T(2,128)(2,1)S(1)} %get-tuple-element.154), channel_id=2, replica_groups=mesh['context'=32,'tensor'=16] {'context'}, dimensions={0}, use_global_device_ids=true | all-gather | bytes 132 | tf_op jit(solution)/shard_map/all_gather | solution.py:12
  44.3 52.7 %all-gather.10.cloned.1.call-done = bf16[64,128,128]{2,1,0:T(8,128)(2,1)} async-done(((bf16[2,128,128]{2,1,0:T(8,128)(2,1)}), bf16[64,128,128]{2,1,0:T(8,128)(2,1)}) %all-gather.10.cloned.1.call-update) | async-done | bytes 2097168 | tf_op jit(solution)/shard_map/all_gather | solution.py:12
  97.0 36.8 %while.14 = (s32[]{:T(128)}, f32[1,2,128,128]{3,2,1,0:T(8,128)S(1)}, s32[]{:T(128)}, bf16[32,1,2]{0,2,1:T(2,128)(2,1)S(1)}, bf16[32,1,2,128,128]{4,3,2,1,0:T(8,128)(2,1)}, /*index=5*/s32[]{:T(128)}, s32[]{:T(128)}) while((s32[]{:T(128)}, f32[1,2,128,128]{3,2,1,0:T(8,128)S(1)}, s32[]{:T(128)}, bf16[32,1,2]{0,2,1:T(2,128)(2,1)S(1)}, ...), condition=%wide.region_3.4_spmd.clone, body=%wide.region_2.3_spmd.clone.sunk | while | flops 163846 | bytes 327829 | solution.py:29
  98.3 0.9 fusion.25
  99.5 0.9 fusion.25
  100.6 0.9 fusion.25
  101.8 0.9 fusion.25
  102.9 0.9 fusion.25
  104.1 0.9 fusion.25
  105.2 0.9 fusion.25
  106.4 0.9 fusion.25
  107.5 0.9 fusion.25
  108.7 0.9 fusion.25
  109.8 0.9 fusion.25
  111.0 0.9 fusion.25
  112.1 0.9 fusion.25
  113.3 0.9 fusion.25
  114.4 0.9 fusion.25
  115.6 0.9 fusion.25
  116.7 0.9 fusion.25
  119.0 0.9 fusion.25
  121.3 0.9 fusion.25
  122.5 0.9 fusion.25
  124.8 0.9 fusion.25
  128.2 0.9 fusion.25
  130.5 0.9 fusion.25
  134.2 1.0 multiply_reduce_fusion
  136.1 49.7 %all-gather.8.cloned.1.call-done = bf16[4096,512]{1,0:T(8,128)(2,1)} async-done(((bf16[128,512]{1,0:T(8,128)(2,1)}), bf16[4096,512]{1,0:T(8,128)(2,1)}) %all-gather.8.cloned.1.call-update) | async-done | bytes 4194320 | tf_op jit(solution)/shard_map/all_gather | solution.py:79
  185.8 48.4 %all-gather.6.cloned.1.call-done = bf16[512,4096]{0,1:T(8,128)(2,1)} async-done(((bf16[512,256]{0,1:T(8,128)(2,1)}), bf16[512,4096]{0,1:T(8,128)(2,1)}) %all-gather.6.cloned.1.call-update) | async-done | bytes 4194320 | tf_op jit(solution)/shard_map/all_gather | solution.py:76
  234.3 6.6 %fusion.3 = bf16[1,512,512]{2,1,0:T(8,128)(2,1)} fusion(bf16[512,4096]{0,1:T(8,128)(2,1)} %all-gather.6.cloned.1.call-done, bf16[4096,512]{1,0:T(8,128)(2,1)} %all-gather.8.cloned.1.call-done, bf16[1,512,512]{2,1,0:T(8,128)(2,1)S(1)} %copy-done.2), kind=kOutput, calls=%fused_computation.8 | convolution fusion | flops 2148270080 | bytes 9437184 | tf_op jit(solution)/shard_map/dot_general | solution.py:77
  (140 shorter events, 19.9 us)
Async XLA Ops:
  6.5 37.7 %copy-start = (bf16[1,512,256]{2,1,0:T(8,128)(2,1)S(1)}, bf16[1,512,256]{2,1,0:T(8,128)(2,1)}, u32[]{:S(2)}) copy-start(bf16[1,512,256]{2,1,0:T(8,128)(2,1)} %param.10) | copy-start | bytes 786436
  6.5 90.4 %all-gather.10.cloned.1.call-start = ((), (), s32[]{:S(2)}) async-start(), calls=%async_computation.2 | async-start | bytes 2162688 | tf_op jit(solution)/shard_map/all_gather | solution.py:12
  11.8 174.0 %all-gather.8.cloned.1.call-start = ((), (), s32[]{:S(2)}) async-start(), calls=%async_computation.1 | async-start | bytes 4325376 | tf_op jit(solution)/shard_map/all_gather | solution.py:79
  12.6 221.7 %all-gather.6.cloned.1.call-start = ((), (), s32[]{:S(2)}) async-start(), calls=%async_computation | async-start | bytes 4456448 | tf_op jit(solution)/shard_map/all_gather | solution.py:76
  134.2 1.1 copy-start.1
  134.2 100.1 %copy-start.2 = (bf16[1,512,512]{2,1,0:T(8,128)(2,1)S(1)}, bf16[1,512,512]{2,1,0:T(8,128)(2,1)}, u32[]{:S(2)}) copy-start(bf16[1,512,512]{2,1,0:T(8,128)(2,1)} %param.17) | copy-start | bytes 1572868
Sparse Core Ops, SparseCore 0:
  11.9 85.0 all-gather.9
  100.1 85.6 all-gather.7
  187.9 46.2 all-gather.5
where the time goes:
time: 249 us; the launch traced here: 247 us
  waiting for transfers between devices  152 us (61%)
  other arithmetic  33 us (13%)
  blocking collectives  31.4 us (13%)
  between operations  13.2 us (5%)
  matrix products  8.93 us (4%)
  local copies, waits for them, and re-layouts  8.36 us (3%)
    all_gather x1, waiting for transfers between devices, prefix_2(): lax.all_gather(part.astype(kind), axis)  52.7 us
    all_gather x1, waiting for transfers between devices, local(): lax.all_gather(out_weight, 'context', axis=0, tiled=True)  49.7 us
    all_gather x1, waiting for transfers between devices, local(): all_heads = lax.all_gather(normed, 'tensor', axis=1, tiled=True)  48.4 us
    all_gather x1, blocking collectives, prefix_2(): lax.all_gather(part.astype(kind), axis)  31.4 us
    select_n x32, other arithmetic, lap(): return jax.tree.map(lambda a, b: jnp.where(reached, a, b), new, before)  29.7 us
    dot_general x1, matrix products, local(): jnp.dot(all_heads, lax.all_gather(out_weight, 'context', axis=0, tiled=Tr...  6.61 us
    dynamic_slice x64, local copies, waits for them, and re-layouts, lap(): part[k].astype(own.dtype)  6.03 us
  transfers between devices with their start and end apart: 3, of which 3 were waited for; matrix products, arithmetic and copies ran while one was open for 16% of the time, Pallas kernels for 0%

commit v1 on v0

--- a/solution.py
+++ b/solution.py
@@ -73,7 +73,9 @@
     scale = lax.rsqrt(jnp.mean(mixed * mixed, axis=-1, keepdims=True) + epsilon)
     normed = (mixed * scale * norm_gain.reshape(1, heads, 1, head_size)).astype(jnp.bfloat16)
     normed = normed.transpose(0, 2, 1, 3).reshape(requests * block, width_here)
-    all_heads = lax.all_gather(normed, "tensor", axis=1, tiled=True)
+    all_heads = jnp.concatenate(
+        lax.all_to_all(jnp.stack([normed] * lax.axis_size("tensor")), "tensor", 0, 0), axis=1
+    )
     projected = jnp.dot(
         all_heads,
         lax.all_gather(out_weight, "context", axis=0, tiled=True),

time: 249 us -> 258 us (1.036)
  starting transfers between devices: 0.08 us -> 12 us
  waiting for transfers between devices: 152 us -> 147 us
    all_to_all x0 -> x1, waiting for transfers between devices: none -> 57.2 us  [local(): lax.all_to_all(jnp.stack([normed] * lax.axis_size('tensor')), 'tensor', 0...]
    all_gather x1 -> x0, waiting for transfers between devices: 48.4 us -> none  [local(): all_heads = lax.all_gather(normed, 'tensor', axis=1, tiled=True)]
    all_gather x1, waiting for transfers between devices: 49.7 us -> 36.4 us  [local(): lax.all_gather(out_weight, 'context', axis=0, tiled=True)]
    all_to_all x0 -> x1, starting transfers between devices: none -> 12 us  [local(): lax.all_to_all(jnp.stack([normed] * lax.axis_size('tensor')), 'tensor', 0...]
where the time goes in v1:
time: 258 us; the launch traced here: 257 us
  waiting for transfers between devices  147 us (57%)
  other arithmetic  32.3 us (13%)
  blocking collectives  31.4 us (12%)
  between operations  13.5 us (5%)
  starting transfers between devices  12 us (5%)
  local copies, waits for them, and re-layouts  10.7 us (4%)
  matrix products  8.95 us (3%)
    all_to_all x1, waiting for transfers between devices, local(): lax.all_to_all(jnp.stack([normed] * lax.axis_size('tensor')), 'tensor', 0...  57.2 us
    all_gather x1, waiting for transfers between devices, prefix_2(): lax.all_gather(part.astype(kind), axis)  52.7 us
    all_gather x1, waiting for transfers between devices, local(): lax.all_gather(out_weight, 'context', axis=0, tiled=True)  36.4 us
    all_gather x1, blocking collectives, prefix_2(): lax.all_gather(part.astype(kind), axis)  31.4 us
    select_n x32, other arithmetic, lap(): return jax.tree.map(lambda a, b: jnp.where(reached, a, b), new, before)  29.7 us
    all_to_all x1, starting transfers between devices, local(): lax.all_to_all(jnp.stack([normed] * lax.axis_size('tensor')), 'tensor', 0...  12 us
    dot_general x1, matrix products, local(): jnp.dot(all_heads, lax.all_gather(out_weight, 'context', axis=0, tiled=Tr...  6.61 us
    dynamic_slice x64, local copies, waits for them, and re-layouts, lap(): part[k].astype(own.dtype)  6.03 us
  transfers between devices with their start and end apart: 3, of which 3 were waited for; matrix products, arithmetic and copies ran while one was open for 16% of the time, Pallas kernels for 0%

profile of v1, /device:TPU:1, one launch (start us, length us, event | category | flops | bytes accessed | tf_op | source)
XLA Modules:
  0.0 256.5 jit_solution(4285925678293693236)
XLA Ops:
  8.4 1.1 multiply_convert_fusion.3
  9.5 1.1 copy.45
  12.7 31.4 %all-gather = bf16[32,2,1]{2,1,0:T(2,128)(2,1)S(1)} all-gather(bf16[1,2,1]{2,1,0:T(2,128)(2,1)S(1)} %get-tuple-element.154), channel_id=2, replica_groups=mesh['context'=32,'tensor'=16] {'context'}, dimensions={0}, use_global_device_ids=true | all-gather | bytes 132 | tf_op jit(solution)/shard_map/all_gather | solution.py:12
  44.2 52.7 %all-gather.7.cloned.1.call-done = bf16[64,128,128]{2,1,0:T(8,128)(2,1)} async-done(((bf16[2,128,128]{2,1,0:T(8,128)(2,1)}), bf16[64,128,128]{2,1,0:T(8,128)(2,1)}) %all-gather.7.cloned.1.call-update) | async-done | bytes 2097168 | tf_op jit(solution)/shard_map/all_gather | solution.py:12
  97.0 36.5 %while.14 = (s32[]{:T(128)}, f32[1,2,128,128]{3,2,1,0:T(8,128)S(1)}, s32[]{:T(128)}, bf16[32,1,2]{0,2,1:T(2,128)(2,1)S(1)}, bf16[32,1,2,128,128]{4,3,2,1,0:T(8,128)(2,1)}, /*index=5*/s32[]{:T(128)}, s32[]{:T(128)}) while((s32[]{:T(128)}, f32[1,2,128,128]{3,2,1,0:T(8,128)S(1)}, s32[]{:T(128)}, bf16[32,1,2]{0,2,1:T(2,128)(2,1)S(1)}, ...), condition=%wide.region_3.4_spmd.clone, body=%wide.region_2.3_spmd.clone.sunk | while | flops 163846 | bytes 327821 | solution.py:29
  99.5 0.9 fusion.25
  100.6 0.9 fusion.25
  101.7 0.9 fusion.25
  102.9 0.9 fusion.25
  104.0 0.9 fusion.25
  105.2 0.9 fusion.25
  106.3 0.9 fusion.25
  107.5 0.9 fusion.25
  115.4 0.9 fusion.25
  116.6 0.9 fusion.25
  117.7 0.9 fusion.25
  118.9 0.9 fusion.25
  120.0 0.9 fusion.25
  121.2 0.9 fusion.25
  122.3 0.9 fusion.25
  123.4 0.9 fusion.25
  125.7 0.9 fusion.25
  126.9 0.9 fusion.25
  128.0 0.9 fusion.25
  130.3 0.9 fusion.25
  131.4 0.9 fusion.25
  134.0 1.1 multiply_reduce_fusion
  135.1 2.4 stack.3
  137.5 12.0 %all-to-all-start = ((bf16[16,512,256]{1,2,0:T(8,128)(2,1)}), bf16[16,512,256]{1,2,0:T(8,128)(2,1)}, u32[]{:S(2)}, u32[]{:S(2)}) async-start(bf16[16,512,256]{1,2,0:T(8,128)(2,1)} %stack.3), calls=%async_computation | async-start | bytes 8388608 | tf_op jit(solution)/shard_map/all_to_all | solution.py:77
  149.5 36.4 %all-gather.5.cloned.1.call-done = bf16[4096,512]{1,0:T(8,128)(2,1)} async-done(((bf16[128,512]{1,0:T(8,128)(2,1)}), bf16[4096,512]{1,0:T(8,128)(2,1)}) %all-gather.5.cloned.1.call-update) | async-done | bytes 4194320 | tf_op jit(solution)/shard_map/all_gather | solution.py:81
  185.8 57.2 %all-to-all-done = bf16[16,512,256]{1,2,0:T(8,128)(2,1)} async-done(((bf16[16,512,256]{1,2,0:T(8,128)(2,1)}), bf16[16,512,256]{1,2,0:T(8,128)(2,1)}, u32[]{:S(2)}, u32[]{:S(2)}) %all-to-all-start) | async-done | bytes 4194336 | tf_op jit(solution)/shard_map/all_to_all | solution.py:77
  243.1 6.6 %fusion.3 = bf16[1,512,512]{2,1,0:T(8,128)(2,1)} fusion(bf16[512,4096]{0,1:T(8,128)(2,1)} %bitcast.17, bf16[4096,512]{1,0:T(8,128)(2,1)} %all-gather.5.cloned.1.call-done, bf16[1,512,512]{2,1,0:T(8,128)(2,1)S(1)} %copy-done.2), kind=kOutput, calls=%fused_computation.8 | convolution fusion | flops 2148270080 | bytes 9437184 | tf_op jit(solution)/shard_map/dot_general | solution.py:79
  (140 shorter events, 21.0 us)
Async XLA Ops:
  6.5 37.6 %copy-start = (bf16[1,512,256]{2,1,0:T(8,128)(2,1)S(1)}, bf16[1,512,256]{2,1,0:T(8,128)(2,1)}, u32[]{:S(2)}) copy-start(bf16[1,512,256]{2,1,0:T(8,128)(2,1)} %param.10) | copy-start | bytes 786436
  6.5 90.4 %all-gather.7.cloned.1.call-start = ((), (), s32[]{:S(2)}) async-start(), calls=%async_computation.2 | async-start | bytes 2162688 | tf_op jit(solution)/shard_map/all_gather | solution.py:12
  11.8 174.0 %all-gather.5.cloned.1.call-start = ((), (), s32[]{:S(2)}) async-start(), calls=%async_computation.1 | async-start | bytes 4325376 | tf_op jit(solution)/shard_map/all_gather | solution.py:81
  133.9 1.1 copy-start.1
  137.5 105.6 %copy-start.2 = (bf16[1,512,512]{2,1,0:T(8,128)(2,1)S(1)}, bf16[1,512,512]{2,1,0:T(8,128)(2,1)}, u32[]{:S(2)}) copy-start(bf16[1,512,512]{2,1,0:T(8,128)(2,1)} %param.17) | copy-start | bytes 1572868
  137.5 105.5 %all-to-all-start = ((bf16[16,512,256]{1,2,0:T(8,128)(2,1)}), bf16[16,512,256]{1,2,0:T(8,128)(2,1)}, u32[]{:S(2)}, u32[]{:S(2)}) async-start(bf16[16,512,256]{1,2,0:T(8,128)(2,1)} %stack.3), calls=%async_computation | async-start | bytes 8388608 | tf_op jit(solution)/shard_map/all_to_all | solution.py:77
Sparse Core Ops, SparseCore 0:
  11.9 85.0 all-gather.6
  100.1 85.6 all-gather.4
